TPU v7x, 32 devices: a whole 2x2x4 slice. The times are simulated.
32 devices in a mesh: az: 8 (over y, x, core), ax: 4 (over z).
Axes of the slice: x: 2, y: 2, z: 4, core: 2. Of those that a mesh axis runs over, the one named last changes fastest.
Arguments:
- step_start: float32 [5, 16, 512, 2048], P(None, None, 'ax', 'az'), may hold values from -3 to 12, as said below
- section_state: float32 [5, 16, 512, 2048], P(None, None, 'ax', 'az'), may hold values from -3 to 12, as said below
- near_rows: int32 [512], P('ax'), may hold values from 1 to 4
- cutoff: int32 [4, 512], P(None, 'ax'), may hold values from 64 to 511
- gore_map: int32 [512, 2048], P('ax', 'az'), may hold values from 0 to 80, as said below
Outputs:
- new_state: float32 [5, 16, 512, 2048], P(None, None, 'ax', 'az')
- gore_loads: float32 [80], replicated
Inputs may be any that keep to these rules, and one draw needn't show every extreme that they name: `step_start`: every cell holds density, momentum and total energy of a gas state whose density and pressure lie between 0.5 and 2 and whose velocity components lie within 1.5 in magnitude. `section_state`: every cell holds density, momentum and total energy of a gas state whose density and pressure lie between 0.5 and 2 and whose velocity components lie within 1.5 in magnitude. `gore_map`: each axial station is either entirely gap, marked 80, or canopy whose gores run in azimuthal bands.
All inputs are finite; a program needn't handle non-finite values.
Results may differ from a plain program's by a relative error of at most 0.000077.
Values sent between devices are 32-bit elements; how exact they have to be, the bound alone decides.
A program may use at most 192 MiB of HBM per device.

v0:
```python
import math

import jax
import jax.numpy as jnp
from jax import lax
from jax.sharding import PartitionSpec as P

NA = 2048
NF = 4
GORES = 80


HEAT_RATIO = 1.4
WEIGHT_EPSILON = 1e-06
INNER_RADIUS = 24.0
RADIAL_STEP = 0.5
AXIAL_STEP = 0.5
TIME_STEP = 0.01
SECTION_KEEP = 1.0 / 3.0
SECTION_GAIN = 2.0 / 3.0


def extended(cells, sides, width):
    for axis, dim in sides:
        count = lax.axis_size(axis)
        head = lax.slice_in_dim(cells, 0, width, axis=dim)
        tail = lax.slice_in_dim(cells, cells.shape[dim] - width, cells.shape[dim], axis=dim)
        cells = jnp.concatenate(
            [
                lax.ppermute(tail, axis, [(i, (i + 1) % count) for i in range(count)]),
                cells,
                lax.ppermute(head, axis, [((i + 1) % count, i) for i in range(count)]),
            ],
            axis=dim,
        )
    return cells


def slice_along(values, along_dim, start_at, length):
    return lax.slice_in_dim(values, start_at, start_at + length, axis=along_dim)


def pressure_of(conserved):
    density = conserved[0]
    kinetic = (
        0.5
        * (conserved[1] * conserved[1] + conserved[2] * conserved[2] + conserved[3] * conserved[3])
        / density
    )
    return (HEAT_RATIO - 1.0) * (conserved[4] - kinetic)


def cell_fluxes(conserved, normal):
    density = conserved[0]
    velocity = conserved[normal] / density
    pressure = pressure_of(conserved)
    flux_parts = [
        conserved[0] * velocity,
        conserved[1] * velocity,
        conserved[2] * velocity,
        conserved[3] * velocity,
        (conserved[4] + pressure) * velocity,
    ]
    flux_parts[normal] = flux_parts[normal] + pressure
    wave_speed = jnp.abs(velocity) + jnp.sqrt(HEAT_RATIO * pressure / density)
    return (jnp.stack(flux_parts), wave_speed)


def weno_side(far_left, near_left, centre, near_right, far_right):
    cand_one = (2.0 * far_left - 7.0 * near_left + 11.0 * centre) / 6.0
    cand_two = (-near_left + 5.0 * centre + 2.0 * near_right) / 6.0
    cand_three = (2.0 * centre + 5.0 * near_right - far_right) / 6.0
    smooth_one = 13.0 / 12.0 * jnp.square(far_left - 2.0 * near_left + centre) + 0.25 * jnp.square(
        far_left - 4.0 * near_left + 3.0 * centre
    )
    smooth_two = 13.0 / 12.0 * jnp.square(
        near_left - 2.0 * centre + near_right
    ) + 0.25 * jnp.square(near_left - near_right)
    smooth_three = 13.0 / 12.0 * jnp.square(
        centre - 2.0 * near_right + far_right
    ) + 0.25 * jnp.square(3.0 * centre - 4.0 * near_right + far_right)
    weight_one = 0.1 / jnp.square(WEIGHT_EPSILON + smooth_one)
    weight_two = 0.6 / jnp.square(WEIGHT_EPSILON + smooth_two)
    weight_three = 0.3 / jnp.square(WEIGHT_EPSILON + smooth_three)
    weight_sum = weight_one + weight_two + weight_three
    return (weight_one * cand_one + weight_two * cand_two + weight_three * cand_three) / weight_sum


def face_fluxes(padded, along_dim, normal):
    face_count = padded.shape[along_dim] - 5
    flux_cells, wave_speed = cell_fluxes(padded, normal)
    damping = jnp.maximum(
        slice_along(wave_speed, along_dim - 1, 2, face_count),
        slice_along(wave_speed, along_dim - 1, 3, face_count),
    )[None]

    def plus_part(offset):
        return 0.5 * (
            slice_along(flux_cells, along_dim, 2 + offset, face_count)
            + damping * slice_along(padded, along_dim, 2 + offset, face_count)
        )

    def minus_part(offset):
        return 0.5 * (
            slice_along(flux_cells, along_dim, 2 + offset, face_count)
            - damping * slice_along(padded, along_dim, 2 + offset, face_count)
        )

    return weno_side(
        plus_part(-2), plus_part(-1), plus_part(0), plus_part(1), plus_part(2)
    ) + weno_side(minus_part(3), minus_part(2), minus_part(1), minus_part(0), minus_part(-1))


def cell_difference(face_values, along_dim):
    cell_count = face_values.shape[along_dim] - 1
    return slice_along(face_values, along_dim, 1, cell_count) - slice_along(
        face_values, along_dim, 0, cell_count
    )


def rate_of(cycle_padded, line_padded):
    interior = cycle_padded[:, :, :, 3:-3]
    row_count = interior.shape[1]
    radial_padded = jnp.pad(interior, ((0, 0), (3, 3), (0, 0), (0, 0)), mode="edge")
    face_radius = INNER_RADIUS + RADIAL_STEP * jnp.arange(row_count + 1, dtype=jnp.float32)
    cell_radius = INNER_RADIUS + RADIAL_STEP * (jnp.arange(row_count, dtype=jnp.float32) + 0.5)
    radial_faces = face_fluxes(radial_padded, 1, 1) * face_radius[None, :, None, None]
    radial_term = (
        cell_difference(radial_faces, 1) / (RADIAL_STEP * cell_radius)[None, :, None, None]
    )
    cycle_term = (
        cell_difference(face_fluxes(cycle_padded, 3, 2), 3)
        / (cell_radius * (2.0 * math.pi / NA))[None, :, None, None]
    )
    line_term = cell_difference(face_fluxes(line_padded, 2, 3), 2) / AXIAL_STEP
    pressure = pressure_of(interior)
    swirl_speed = interior[2] / interior[0]
    radius_cells = cell_radius[:, None, None]
    source_radial = (interior[2] * swirl_speed + pressure) / radius_cells
    source_swirl = -interior[1] * swirl_speed / radius_cells
    zero_field = jnp.zeros_like(pressure)
    sources = jnp.stack([zero_field, source_radial, source_swirl, zero_field, zero_field])
    return (interior, sources - radial_term - cycle_term - line_term)


def close_ends(padded, line_index, line_count):
    at_first = line_index == 0
    at_last = line_index == line_count - 1
    lower_rim = jnp.where(at_first, jnp.repeat(padded[:, :, 3:4], 3, axis=2), padded[:, :, :3])
    upper_rim = jnp.where(at_last, jnp.repeat(padded[:, :, -4:-3], 3, axis=2), padded[:, :, -3:])
    return jnp.concatenate([lower_rim, padded[:, :, 3:-3], upper_rim], axis=2)


def fourier_basis(positions, mode_index):
    phase_index = positions[:, None] * mode_index[None, :] % NA
    angles = 2.0 * math.pi / NA * phase_index.astype(jnp.float32)
    return jnp.concatenate([jnp.cos(angles), jnp.sin(angles)], axis=1)


def per_device(step_start, section_state, near_rows, cutoff, gore_map):
    stations = section_state.shape[2]
    cycle_cells = section_state.shape[3]
    line_count = lax.axis_size("ax")
    cycle_index = lax.axis_index("az")
    line_index = lax.axis_index("ax")
    both_sides = extended(section_state, (("az", 3), ("ax", 2)), 3)
    cycle_padded = both_sides[:, :, 3:-3, :]
    line_padded = close_ends(both_sides[:, :, :, 3:-3], line_index, line_count)
    interior, tendency = rate_of(cycle_padded, line_padded)
    updated = SECTION_KEEP * step_start + SECTION_GAIN * (interior + TIME_STEP * tendency)
    near_cycles = updated[:, :NF].reshape(5, NF * stations, cycle_cells)
    cutoff_rows = cutoff.reshape(-1)
    chosen_rows = (jnp.arange(NF, dtype=jnp.int32)[:, None] < near_rows[None, :]).reshape(-1)
    quarter = NA // 4
    mode_index = jnp.arange(quarter, dtype=jnp.int32)
    column_modes = jnp.concatenate([mode_index, mode_index])
    column_weight = jnp.concatenate(
        [jnp.where(mode_index == 0, 1.0 / NA, 2.0 / NA), jnp.full((quarter,), 2.0 / NA)]
    ).astype(jnp.float32)
    local_basis = fourier_basis(
        cycle_index * cycle_cells + jnp.arange(cycle_cells, dtype=jnp.int32), mode_index
    )
    partial_modes = jnp.einsum(
        "frn,nc->frc", near_cycles, local_basis, precision=lax.Precision.HIGHEST
    )
    coefficients = lax.psum(partial_modes, "az")
    mode_gains = jnp.where(
        column_modes[None, :] < cutoff_rows[:, None], column_weight[None, :], 0.0
    )
    rebuilt = jnp.einsum(
        "frc,nc->frn", coefficients * mode_gains[None], local_basis, precision=lax.Precision.HIGHEST
    )
    near_new = jnp.where(chosen_rows[None, :, None], rebuilt, near_cycles)
    new_state = jnp.concatenate(
        [near_new.reshape(5, NF, stations, cycle_cells), updated[:, NF:]], axis=1
    )
    canopy = section_state.shape[1] // 2
    pressure_jump = pressure_of(section_state[:, canopy - 1]) - pressure_of(
        section_state[:, canopy + 1]
    )
    total_stations = stations * line_count
    global_station = line_index * stations + jnp.arange(stations, dtype=jnp.int32)
    axial_ramp = 1.0 + 2.0 * global_station.astype(jnp.float32) / total_stations
    weighted = pressure_jump * axial_ramp[:, None] * (1.0 / math.sqrt(total_stations * NA / GORES))
    gore_index = jnp.arange(GORES, dtype=jnp.int32)
    partial_loads = jnp.sum(
        jnp.where(gore_map[None] == gore_index[:, None, None], weighted[None], 0.0), axis=(1, 2)
    )
    gore_loads = lax.psum(partial_loads, ("az", "ax"))
    return (new_state, gore_loads)


def solution(mesh):
    in_specs = (
        P(None, None, "ax", "az"),
        P(None, None, "ax", "az"),
        P("ax"),
        P(None, "ax"),
        P("ax", "az"),
    )
    out_specs = (P(None, None, "ax", "az"), P())
    return jax.shard_map(
        per_device, mesh=mesh, in_specs=in_specs, out_specs=out_specs, check_vma=False
    )
```

profile of v0, /device:TPU:0, one launch (start us, length us, event | category | flops | bytes accessed | tf_op | source)
XLA Modules:
  0.0 600.7 jit_solution(18224234876430811806)
XLA Ops:
  7.2 9.7 %fusion.97 = (f32[5,16,128,3]{3,2,1,0:T(8,128)}, f32[5,16,128,3]{3,2,1,0:T(8,128)}) fusion(f32[5,16,128,256]{3,2,1,0:T(8,128)} %param.6), kind=kLoop, calls=%fused_computation.208 | loop fusion | bytes 491520 | tf_op jit(solution)/shard_map/slice | solution.py:27
  16.9 3.3 copy.77
  20.7 3.3 copy.78
  24.0 3.0 collective-permute-start.1
  31.2 5.5 pad_maximum_fusion.3
  36.7 2.3 multiply_dynamic-update-slice_fusion.7
  39.0 2.0 fusion.71
  42.0 4.2 slice-done.1
  47.1 3.4 add_dynamic-update-slice_fusion.1
  50.5 2.0 multiply_dynamic-update-slice_fusion.6
  52.5 1.9 multiply_dynamic-update-slice_fusion.5
  54.4 1.6 slice_maximum_fusion.2
  56.1 2.6 add_divide_fusion
  58.7 3.3 fusion.90
  61.9 4.9 multiply_dynamic-update-slice_fusion.4
  66.8 63.5 %add_multiply_fusion.4 = f32[5,17,128,256]{3,2,1,0:T(8,128)} fusion(f32[5,3,128,256]{3,2,1,0:T(8,128)S(1)} %copy-done.10, f32[5,16,128,256]{3,2,1,0:T(8,128)} %param.6, f32[5,22,128,256]{3,2,1,0:T(8,128)} %multiply_dynamic-update-slice_fusion.4, f32[5,3,128,256]{3,2,1,0:T(8,128)S(1)} %copy-done.8, f32[17]{0:T(128)S(1)} %multiply_add_fusion.2, ...), kind=kLoop, calls=%fused_computation.79 | loop fusion | flops 428933120 | bytes 94634048 | tf_op jit(solution)/shard_map/mul | solution.py:127
  131.1 3.1 copy.65
  134.3 3.2 copy.66
  137.4 10.4 %pad_maximum_fusion.2 = f32[5,16,128,262]{3,2,1,0:T(8,128)S(1)} fusion(f32[5,16,128,3]{3,2,1,0:T(8,128)} %copy.66, f32[5,16,128,256]{3,2,1,0:T(8,128)} %param.6, f32[5,16,128,3]{3,2,1,0:T(8,128)} %copy.65), kind=kLoop, calls=%fused_computation.30 | loop fusion | flops 5365760 | bytes 21463040 | tf_op jit(solution)/shard_map/concatenate | solution.py:28
  147.9 3.9 multiply_dynamic-update-slice_fusion.3
  151.8 3.7 fusion.64
  156.8 2.9 pad_maximum_fusion.11
  159.8 2.0 multiply_dynamic-update-slice_fusion.2
  162.8 2.6 add_dynamic-update-slice_fusion
  165.4 1.9 multiply_dynamic-update-slice_fusion.1
  167.3 1.7 slice_maximum_fusion
  169.1 2.4 collective-permute-start.2
  172.2 2.0 collective-permute-start.3
  174.2 2.2 multiply_dynamic-update-slice_fusion
  176.4 98.5 %divide_add_fusion = f32[5,16,128,257]{3,2,1,0:T(8,128)} fusion(f32[5,16,128,3]{3,2,1,0:T(8,128)} %copy.66, f32[5,16,128,256]{3,2,1,0:T(8,128)} %param.6, f32[5,16,128,262]{3,2,1,0:T(8,128)} %multiply_dynamic-update-slice_fusion, f32[5,16,128,3]{3,2,1,0:T(8,128)} %copy.65, f32[16,128,257]{2,1,0:T(8,128)S(1)} %slice_maximum_fusion), kind=kLoop, calls=%fused_computation.31 | loop fusion | flops 402647040 | bytes 86523904 | tf_op jit(solution)/shard_map/add | solution.py:109
  278.2 1.8 copy_select_fusion
  280.1 5.5 pad_maximum_fusion.8
  285.5 1.9 multiply_dynamic-update-slice_fusion.11
  287.5 3.4 fusion.78
  290.9 1.7 multiply_dynamic-update-slice_fusion.10
  292.6 1.6 multiply_dynamic-update-slice_fusion.9
  294.2 6.8 %add_dynamic-update-slice_fusion.2 = (f32[5,16,134,256]{3,2,1,0:T(8,128)}, f32[1,16,134,256]{3,2,1,0:T(8,128)S(1)}) fusion(f32[5,16,134,256]{3,2,1,0:T(8,128)} %multiply_dynamic-update-slice_fusion.9, f32[1,16,134,256]{3,2,1,0:T(8,128)S(1)} %get-tuple-element.17, f32[5,16,134,256]{3,2,1,0:T(8,128)} %copy-done.1), kind=kLoop, calls=%fused_computation.159 | loop fusion | flops 6037504 | bytes 17760256
  301.4 4.0 multiply_dynamic-update-slice_fusion.8
  305.5 69.4 %divide_add_fusion.1 = f32[5,16,129,256]{3,2,1,0:T(8,128)} fusion(f32[5,16,3,256]{3,2,1,0:T(4,128)} %copy_select_fusion, f32[5,16,128,256]{3,2,1,0:T(8,128)S(1)} %bitcast.142, f32[5,16,134,256]{3,2,1,0:T(8,128)} %multiply_dynamic-update-slice_fusion.8, f32[5,16,3,256]{3,2,1,0:T(4,128)S(1)} %copy_select_fusion.1, f32[16,129,256]{2,1,0:T(8,128)S(1)} %slice_maximum_fusion.1), kind=kLoop, calls=%fused_computation.72 | loop fusion | flops 404213760 | bytes 87064576 | tf_op jit(solution)/shard_map/add | solution.py:109
  374.9 34.7 %fusion.50 = f32[5,16,128,256]{3,2,1,0:T(8,128)} fusion(f32[5,16,128,256]{3,2,1,0:T(8,128)} %param.6, f32[5,16,129,256]{3,2,1,0:T(8,128)} %divide_add_fusion.1, f32[5,16,128,257]{3,2,1,0:T(8,128)} %divide_add_fusion, f32[5,17,128,256]{3,2,1,0:T(8,128)} %add_multiply_fusion.4, f32[1,16,128,256]{3,2,1,0:T(8,128)} %get-tuple-element.21, ...), kind=kLoop, calls=%fused_computation.92 | loop fusion | flops 44564480 | bytes 98566312 | tf_op jit(solution)/shard_map/add | solution.py:170
  409.6 2.0 slice.566
  413.1 11.1 %fusion.82 = f32[5,512,1024]{2,1,0:T(8,128)} fusion(f32[5,512,256]{2,1,0:T(8,128)S(1)} %bitcast.145, f32[256,512]{1,0:T(8,128)S(1)} %copy-done.13, f32[256,512]{1,0:T(8,128)S(1)} %copy-done.12), kind=kOutput, calls=%fused_computation.172 | convolution fusion | flops 8053325824 | bytes 14155776 | tf_op jit(solution)/shard_map/frn,nc->frc/dot_general | solution.py:183
  424.3 1.5 fusion.91
  427.1 39.4 %psum.15 = f32[80]{0:T(128)} all-reduce(f32[80]{0:T(128)S(1)} %select_reduce_fusion), channel_id=1, replica_groups=mesh['az'=8,'ax'=4] {'az','ax'}, use_global_device_ids=true, to_apply=%region_2.3 | all-reduce | flops 80 | bytes 640 | tf_op jit(solution)/shard_map/psum | solution.py:209
  466.5 1.5 compare_select_fusion
  468.0 105.7 %all-reduce.3.cloned.1.call-done = f32[5,512,1024]{2,1,0:T(8,128)} async-done(((f32[5,512,1024]{2,1,0:T(8,128)}), f32[5,512,1024]{2,1,0:T(8,128)}) %all-reduce.3.cloned.1.call-update) | async-done | bytes 10485776 | tf_op jit(solution)/shard_map/psum | solution.py:186
  573.8 13.2 %fusion.79 = f32[5,512,256]{2,1,0:T(8,128)} fusion(f32[5,512,256]{2,1,0:T(8,128)} %bitcast.146, f32[5,512,1024]{2,1,0:T(8,128)} %all-reduce.3.cloned.1.call-done, f32[512,1024]{1,0:T(8,128)} %compare_select_fusion, pred[512]{0:T(512)(128)(4,1)S(1)} %fusion.92, f32[256,512]{1,0:T(8,128)S(1)} %copy-done.14, f32[256,512]{1,0:T(8,128)S(1)} %copy-done.12), kind=kOutput, calls=%fused_computation.170 | convolution fusion | flops 8056602624 | bytes 18874880 | tf_op jit(solution)/shard_map/frc,nc->frn/dot_general | solution.py:190
  587.0 6.6 %pad_maximum_fusion.9 = f32[5,16,128,256]{3,2,1,0:T(8,128)} fusion(f32[5,12,128,256]{3,2,1,0:T(8,128)S(1)} %slice-done.11, f32[5,4,128,256]{3,2,1,0:T(8,128)} %bitcast.147), kind=kLoop, calls=%fused_computation.99 | loop fusion | flops 2621440 | bytes 20971520 | tf_op jit(solution)/shard_map/concatenate | solution.py:194
  (99 shorter events, 16.9 us)
Async XLA Ops:
  7.2 566.6 %all-reduce.3.cloned.1.call-start = ((), (), s32[]{:S(2)}) async-start(), calls=%async_computation | async-start | bytes 20971520 | tf_op jit(solution)/shard_map/psum | solution.py:186
  20.2 110.9 %collective-permute-start = (f32[5,16,128,3]{2,1,3,0:T(8,128)S(1)}, f32[5,16,128,3]{2,1,3,0:T(8,128)S(1)}, u32[]{:S(2)}, u32[]{:S(2)}) collective-permute-start(f32[5,16,128,3]{2,1,3,0:T(8,128)S(1)} %copy.77), channel_id=1, source_target_pairs={{0,4},{4,8},{8,12},{12,16},{16,20},{20,24},{24,28},{28,0},{1,5},{5... | collective-permute-start | bytes 368648 | tf_op jit(solution)/shard_map/ppermute | solution.py:30
  24.0 110.3 %collective-permute-start.1 = (f32[5,16,128,3]{2,1,3,0:T(8,128)S(1)}, f32[5,16,128,3]{2,1,3,0:T(8,128)S(1)}, u32[]{:S(2)}, u32[]{:S(2)}) collective-permute-start(f32[5,16,128,3]{2,1,3,0:T(8,128)S(1)} %copy.78), channel_id=1, source_target_pairs={{4,0},{8,4},{12,8},{16,12},{20,16},{24,20},{28,24},{0,28},{5,1},{9... | collective-permute-start | bytes 368648 | tf_op jit(solution)/shard_map/ppermute | solution.py:32
  28.6 1.3 copy-start.7
  29.9 1.3 copy-start.9
  36.7 15.8 %copy-start = (f32[5,22,128,256]{3,2,1,0:T(8,128)}, f32[5,22,128,256]{3,2,1,0:T(8,128)S(1)}, u32[]{:S(2)}) copy-start(f32[5,22,128,256]{3,2,1,0:T(8,128)S(1)} %pad_maximum_fusion.3) | copy-start | bytes 43253764
  36.7 5.3 slice-start
  36.7 9.5 %slice-start.1 = ((s8[10485760]{0:T(1024)(128)(4,1)}), s8[4194304]{0:T(1024)(128)(4,1)S(1)}, s32[]{:S(2)}) async-start(s8[10485760]{0:T(1024)(128)(4,1)} %bitcast.137), calls=%async_computation.2 | async-start | bytes 8388608
  39.0 7.9 %slice-start.2 = ((s8[10485760]{0:T(1024)(128)(4,1)}), s8[2097152]{0:T(1024)(128)(4,1)S(1)}, s32[]{:S(2)}) async-start(s8[10485760]{0:T(1024)(128)(4,1)} %bitcast.137), calls=%async_computation.3 | async-start | bytes 4194304
  58.7 8.2 %copy-start.8 = (f32[5,3,128,256]{3,2,1,0:T(8,128)S(1)}, f32[5,3,128,256]{3,2,1,0:T(8,128)}, u32[]{:S(2)}) copy-start(f32[5,3,128,256]{3,2,1,0:T(8,128)} %copy-done.7) | copy-start | bytes 5898244
  58.7 8.2 %copy-start.10 = (f32[5,3,128,256]{3,2,1,0:T(8,128)S(1)}, f32[5,3,128,256]{3,2,1,0:T(8,128)}, u32[]{:S(2)}) copy-start(f32[5,3,128,256]{3,2,1,0:T(8,128)} %copy-done.9) | copy-start | bytes 5898244
  147.9 7.7 %slice-start.3 = ((s8[10485760]{0:T(1024)(128)(4,1)}), s8[4194304]{0:T(1024)(128)(4,1)S(1)}, s32[]{:S(2)}) async-start(s8[10485760]{0:T(1024)(128)(4,1)} %bitcast.139), calls=%async_computation.4 | async-start | bytes 8388608
  147.9 7.7 %slice-start.4 = ((s8[10485760]{0:T(1024)(128)(4,1)}), s8[2097152]{0:T(1024)(128)(4,1)S(1)}, s32[]{:S(2)}) async-start(s8[10485760]{0:T(1024)(128)(4,1)} %bitcast.139), calls=%async_computation.5 | async-start | bytes 4194304
  147.9 7.7 %slice-start.9 = ((s8[5242880]{0:T(1024)(128)(4,1)}), s8[4194304]{0:T(1024)(128)(4,1)S(1)}, s32[]{:S(2)}) async-start(s8[5242880]{0:T(1024)(128)(4,1)} %bitcast.143), calls=%async_computation.10 | async-start | bytes 8388608
  151.8 4.8 slice-start.5
  151.8 5.0 slice-start.10
  156.8 2.9 copy-start.2
  159.8 3.0 copy-start.3
  162.8 4.5 copy-start.4
  165.4 3.6 copy-start.16
  165.4 6.0 %copy-start.15 = (f32[5,16,3,262]{3,2,1,0:T(4,128)S(1)}, f32[5,16,3,262]{3,2,1,0:T(4,128)}, u32[]{:S(2)}) copy-start(f32[5,16,3,262]{3,2,1,0:T(4,128)} %get-tuple-element.19) | copy-start | bytes 754564
  169.1 105.8 %collective-permute-start.2 = (f32[5,16,3,262]{3,1,2,0:T(8,128)S(1)}, f32[5,16,3,262]{3,1,2,0:T(8,128)}, u32[]{:S(2)}, u32[]{:S(2)}) collective-permute-start(f32[5,16,3,262]{3,1,2,0:T(8,128)S(1)} %copy.72), channel_id=1, source_target_pairs={{0,1},{1,2},{2,3},{3,0},{4,5},{5,6},{6,7},{7,4},{8,9},{9,10},{10,1... | collective-permute-start | bytes 754568 | tf_op jit(solution)/shard_map/ppermute | solution.py:30
  172.2 104.9 %collective-permute-start.3 = (f32[5,16,3,262]{3,1,2,0:T(8,128)}, f32[5,16,3,262]{3,1,2,0:T(8,128)}, u32[]{:S(2)}, u32[]{:S(2)}) collective-permute-start(f32[5,16,3,262]{3,1,2,0:T(8,128)} %copy.75), channel_id=1, source_target_pairs={{1,0},{2,1},{3,2},{0,3},{5,4},{6,5},{7,6},{4,7},{9,8},{10,9},{11,1... | collective-permute-start | bytes 754568 | tf_op jit(solution)/shard_map/ppermute | solution.py:32
  285.5 7.1 %copy-start.1 = (f32[5,16,134,256]{3,2,1,0:T(8,128)}, f32[5,16,134,256]{3,2,1,0:T(8,128)S(1)}, u32[]{:S(2)}) copy-start(f32[5,16,134,256]{3,2,1,0:T(8,128)S(1)} %pad_maximum_fusion.8) | copy-start | bytes 32931844
  294.2 6.8 %copy-start.6 = (f32[16,134,256]{2,1,0:T(8,128)S(1)}, f32[16,134,256]{2,1,0:T(8,128)}, u32[]{:S(2)}) copy-start(f32[16,134,256]{2,1,0:T(8,128)} %fusion.78) | copy-start | bytes 6586372
  294.2 11.2 %slice-start.6 = ((s8[10485760]{0:T(1024)(128)(4,1)}), s8[4194304]{0:T(1024)(128)(4,1)S(1)}, s32[]{:S(2)}) async-start(s8[10485760]{0:T(1024)(128)(4,1)} %bitcast.141), calls=%async_computation.7 | async-start | bytes 8388608
  294.2 11.2 %slice-start.7 = ((s8[10485760]{0:T(1024)(128)(4,1)}), s8[4194304]{0:T(1024)(128)(4,1)S(1)}, s32[]{:S(2)}) async-start(s8[10485760]{0:T(1024)(128)(4,1)} %bitcast.141), calls=%async_computation.8 | async-start | bytes 8388608
  301.1 4.4 slice-start.8
  305.5 69.4 %copy-start.11 = (f32[1,16,128,256]{3,2,1,0:T(8,128)S(1)}, f32[1,16,128,256]{3,2,1,0:T(8,128)}, u32[]{:S(2)}) copy-start(f32[1,16,128,256]{3,2,1,0:T(8,128)} %get-tuple-element.20) | copy-start | bytes 6291460
  374.9 38.2 %copy-start.12 = (f32[256,512]{1,0:T(8,128)S(1)}, f32[256,512]{1,0:T(8,128)}, u32[]{:S(2)}) copy-start(f32[256,512]{1,0:T(8,128)} %get-tuple-element.28) | copy-start | bytes 1572868
  374.9 38.2 %copy-start.13 = (f32[256,512]{1,0:T(8,128)S(1)}, f32[256,512]{1,0:T(8,128)}, u32[]{:S(2)}) copy-start(f32[256,512]{1,0:T(8,128)} %get-tuple-element.29) | copy-start | bytes 1572868
  411.6 1.5 copy-start.5
  413.1 12.7 %copy-start.17 = (s32[128,256]{1,0:T(8,128)S(1)}, s32[128,256]{1,0:T(8,128)}, u32[]{:S(2)}) copy-start(s32[128,256]{1,0:T(8,128)} %param.9) | copy-start | bytes 393220
  413.1 53.4 %copy-start.19 = (s32[128]{0:T(128)S(1)}, s32[128]{0:T(128)}, u32[]{:S(2)}) copy-start(s32[128]{0:T(128)} %param.7) | copy-start | bytes 1540
  413.1 53.4 %copy-start.18 = (s32[4,128]{1,0:T(4,128)S(1)}, s32[4,128]{1,0:T(4,128)}, u32[]{:S(2)}) copy-start(s32[4,128]{1,0:T(4,128)} %param.8) | copy-start | bytes 6148
  424.3 149.5 %copy-start.14 = (f32[256,512]{1,0:T(8,128)S(1)}, f32[256,512]{1,0:T(8,128)}, u32[]{:S(2)}) copy-start(f32[256,512]{1,0:T(8,128)} %get-tuple-element.29) | copy-start | bytes 1572868
  573.8 13.2 %slice-start.11 = ((f32[5,16,128,256]{3,2,1,0:T(8,128)}), f32[5,12,128,256]{3,2,1,0:T(8,128)S(1)}, s32[]{:S(2)}) async-start(f32[5,16,128,256]{3,2,1,0:T(8,128)} %fusion.50), calls=%async_computation.12 | async-start | bytes 15728640 | tf_op jit(solution)/shard_map/slice | solution.py:195
Sparse Core Ops, SparseCore 0:
  424.4 149.3 all-reduce.2
where the time goes:
time: 604 us; the launch traced here: 601 us
  other arithmetic  366 us (61%)
  waiting for transfers between devices  106 us (18%)
  local copies, waits for them, and re-layouts  42.4 us (7%)
  blocking collectives  39.4 us (7%)
  matrix products  24.3 us (4%)
  between operations  14.7 us (2%)
  starting transfers between devices  7.9 us (1%)
    add x2, other arithmetic, face_fluxes(): weno_side(plus_part(-2), plus_part(-1), plus_part(0), plus_part(1), plus_...  168 us
    psum x1, waiting for transfers between devices, per_device(): coefficients = lax.psum(partial_modes, 'az')  106 us
    mul x1, other arithmetic, rate_of(): face_fluxes(radial_padded, 1, 1) * face_radius[None, :, None, None]  63.5 us
    psum x1, blocking collectives, per_device(): gore_loads = lax.psum(partial_loads, ('az', 'ax'))  39.4 us
    add x1, other arithmetic, per_device(): SECTION_KEEP * step_start + SECTION_GAIN * (interior + TIME_STEP * tendency)  34.7 us
    unnamed x16, other arithmetic  32.2 us
    unnamed x64, local copies, waits for them, and re-layouts  18.7 us
    dot_general x1, matrix products, per_device(): jnp.einsum('frc,nc->frn', coefficients * mode_gains[None], local_basis, p...  13.2 us
  transfers between devices with their start and end apart: 5, of which 1 were waited for; matrix products, arithmetic and copies ran while one was open for 35% of the time, Pallas kernels for 0%

commit v1 on v0

v1 whole, which is shorter than its diff:
```python
import functools
import math

import jax
import jax.numpy as jnp
import numpy as np
from jax import lax
from jax.experimental import pallas as pl
from jax.experimental.pallas import tpu as pltpu
from jax.sharding import PartitionSpec as P

NA = 2048
NF = 4
GORES = 80

HEAT_RATIO = 1.4
WEIGHT_EPSILON = 1e-06
INNER_RADIUS = 24.0
RADIAL_STEP = 0.5
AXIAL_STEP = 0.5
TIME_STEP = 0.01
SECTION_KEEP = 1.0 / 3.0
SECTION_GAIN = 2.0 / 3.0

SB = 8
EPS = 3.0 * WEIGHT_EPSILON


def correction(d1, d2, d3, d4):
    e1 = d2 - d1
    e2 = d3 - d2
    e3 = d4 - d3
    h2 = 0.75 * d2
    h3 = 0.75 * d3
    s1 = (e1 * e1 + EPS) + h2 * (d2 + e1)
    s2 = (e2 * e2 + EPS) + h2 * d3
    s3 = (e3 * e3 + EPS) + h3 * (d3 - e3)
    y23 = s2 * s3
    y13 = s1 * s3
    y12 = s1 * s2
    a1 = y23 * y23
    a2 = y13 * y13
    a3 = 3.0 * (y12 * y12)
    den = a1 + 6.0 * a2 + a3
    num = (a1 + a1) * (e1 - e2) + a3 * (e2 - e3)
    return num * pl.reciprocal(den, approx=False)


def face_flux12(df, du, a, fsum):
    au = [a * x for x in du]
    pm2, pm1, p0, p1 = (df[k] + au[k] for k in range(4))
    mm1, m0, m1, m2 = (df[k] - au[k] for k in range(1, 5))
    cp = correction(pm2, pm1, p0, p1)
    cm = correction(m2, m1, m0, mm1)
    return 6.0 * fsum + ((pm1 - m1) - (au[2] + au[2]) + (cp - cm))


def primitives(u):
    rinv = 1.0 / u[0]
    kin = 0.5 * (u[1] * u[1] + u[2] * u[2] + u[3] * u[3]) * rinv
    p = (HEAT_RATIO - 1.0) * (u[4] - kin)
    cs = jnp.sqrt(HEAT_RATIO * p * rinv)
    return rinv, p, cs


def fluxes(u, vel, p, normal):
    f = [u[normal], u[1] * vel, u[2] * vel, u[3] * vel, (u[4] + p) * vel]
    f[normal] = f[normal] + p
    return f


def rk_kernel(cfg, *refs):
    r0, r1, q0, q1, rows_all, nblk, lt, has_alias = cfg
    state, lo, hi, left, right, start = refs[:6]
    out = refs[7] if has_alias else refs[6]
    U, FX, SX, RI, PR, CS, DR, SR, RF, CX, EX, sems = refs[8 if has_alias else 7:]
    nq = q1 - q0
    nr = r1 - r0
    st = nblk * SB
    i = pl.program_id(0)
    lane = lax.broadcasted_iota(jnp.int32, (lt, SB, 128), 2)
    lane1 = lax.broadcasted_iota(jnp.int32, (SB, 128), 1)
    sub = lax.broadcasted_iota(jnp.int32, (lt, SB, 128), 1)

    def axial_faces(c, q, base):
        def ld(ref, k, *ix):
            return ref[(*ix, q, slice(None), pl.ds(base + k, SB), slice(None))]

        uu = [ld(U, k, c) for k in range(-2, 4)]
        ff = [ld(U, k, 3) for k in range(-2, 4)] if c == 0 else [ld(FX, k, c - 1) for k in range(-2, 4)]
        a = jnp.maximum(ld(SX, 0), ld(SX, 1))
        df = [ff[k + 1] - ff[k] for k in range(5)]
        du = [uu[k + 1] - uu[k] for k in range(5)]
        return face_flux12(df, du, a, ff[2] + ff[3])

    @pl.when(i == 0)
    def _():
        copies = []
        for l in range(lt):
            ls = pl.ds(128 * l, 128)
            copies.append(pltpu.make_async_copy(
                state.at[:, pl.ds(q0, nq), :, ls], U.at[:, :, l, pl.ds(SB, st), :], sems.at[3 * l]))
            copies.append(pltpu.make_async_copy(
                lo.at[:, pl.ds(q0, nq), :, ls], U.at[:, :, l, pl.ds(0, SB), :], sems.at[3 * l + 1]))
            copies.append(pltpu.make_async_copy(
                hi.at[:, pl.ds(q0, nq), :, ls], U.at[:, :, l, pl.ds(SB + st, SB), :], sems.at[3 * l + 2]))
        for cp in copies:
            cp.start()
        for cp in copies:
            cp.wait()

        def close_end(at_end, to, end, edge):
            @pl.when(at_end)
            def _():
                def close_row(q, _):
                    for c in range(5):
                        cell = U[c, q, :, pl.ds(end, SB), :][:, edge:edge + 1]
                        U[c, q, :, pl.ds(to, SB), :] = jnp.broadcast_to(cell, (lt, SB, 128))
                    return 0

                lax.fori_loop(0, nq, close_row, 0)

        line = lax.axis_index("ax")
        close_end(line == 0, 0, SB, 0)
        close_end(line == lax.axis_size("ax") - 1, SB + st, st, SB - 1)

        def prim_row(q, _):
            def prim_block(b, _):
                ds = pl.ds(pl.multiple_of(b * SB, SB), SB)
                u = [U[c, q, :, ds, :] for c in range(5)]
                rinv, p, cs = primitives(u)
                vel = u[3] * rinv
                f = fluxes(u, vel, p, 3)
                for c in range(1, 5):
                    FX[c - 1, q, :, ds, :] = f[c]
                SX[q, :, ds, :] = jnp.abs(vel) + cs
                RI[q, :, ds, :] = rinv
                PR[q, :, ds, :] = p
                CS[q, :, ds, :] = cs
                return 0

            return lax.fori_loop(0, nblk + 2, prim_block, 0)

        lax.fori_loop(0, nq, prim_row, 0)

        def first_faces(r, _):
            for c in range(5):
                f = axial_faces(c, r + (r0 - q0), SB - 4)
                CX[c, r] = pltpu.roll(f, 4, 1)
            return 0

        lax.fori_loop(0, nr, first_faces, 0)

    base = pl.multiple_of(i * SB + SB, SB)
    ds = pl.ds(base, SB)

    hs = pl.ds(pl.multiple_of(i * SB, SB), SB)
    u = [left[c, hs, :] for c in range(5)]
    rinv, p, cs = primitives(u)
    vel = u[2] * rinv
    f = fluxes(u, vel, p, 2)
    s = jnp.abs(vel) + cs
    a = jnp.maximum(s, pltpu.roll(s, 127, 1))
    for c in range(5):
        df0 = pltpu.roll(f[c], 127, 1) - f[c]
        du0 = pltpu.roll(u[c], 127, 1) - u[c]
        df = [df0 if k == 0 else pltpu.roll(df0, (-k) % 128, 1) for k in range(-2, 3)]
        du = [du0 if k == 0 else pltpu.roll(du0, (-k) % 128, 1) for k in range(-2, 3)]
        EX[c] = face_flux12(df, du, a, f[c] + pltpu.roll(f[c], 127, 1))

    def radial_flux(q):
        u = [U[c, q, :, ds, :] for c in range(5)]
        vel = u[1] * RI[q, :, ds, :]
        f = fluxes(u, vel, PR[q, :, ds, :], 1)
        return u, f, jnp.abs(vel) + CS[q, :, ds, :]

    ne = nr + 5

    def radial_edge(e, carry):
        u, f = carry[:5], carry[5:10]
        q = jnp.clip(e + (r0 - 3) + 1, 0, rows_all - 1) - q0
        un, fn, sn = radial_flux(q)
        for c in range(5):
            DR[c, 0, e] = fn[c] - f[c]
            DR[c, 1, e] = un[c] - u[c]
            RF[c, e] = fn[c] + f[c]
        SR[e] = jnp.maximum(carry[10], sn)
        return (*un, *fn, sn)

    u, f, s = radial_flux(max(r0 - 3, 0) - q0)
    lax.fori_loop(0, ne, radial_edge, (*u, *f, s))

    def radial_face(c, e):
        df = [DR[c, 0, e + k] for k in range(-2, 3)]
        du = [DR[c, 1, e + k] for k in range(-2, 3)]
        return face_flux12(df, du, SR[e], RF[c, e])

    gain = SECTION_GAIN * TIME_STEP

    def one_row(r, low_faces):
        q = r + (r0 - q0)
        row = (r + r0).astype(jnp.float32)
        radius = INNER_RADIUS + RADIAL_STEP * (row + 0.5)
        rr = 1.0 / jnp.full((1, 1, 128), radius, jnp.float32)
        k_low = (gain / 12.0 / RADIAL_STEP) * (INNER_RADIUS + RADIAL_STEP * row) * rr
        k_up = (gain / 12.0 / RADIAL_STEP) * (INNER_RADIUS + RADIAL_STEP * (row + 1.0)) * rr
        k_cycle = (gain / 12.0 * NA / (2.0 * math.pi)) * rr
        k_line = gain / 12.0 / AXIAL_STEP
        k_src = gain * rr
        lr = r + r0
        uc = []
        for c in range(5):
            halo = jnp.where(
                lane1 < 64,
                pltpu.roll(right[c, hs, :], 125 - 8 * lr, 1),
                pltpu.roll(left[c, hs, :], 125 - 8 * lr, 1),
            )
            uc.append(jnp.concatenate([U[c, q, :, ds, :], halo[None]], axis=0))
        hr, hp, hc = primitives([x[lt:] for x in uc])
        rinv = jnp.concatenate([RI[q, :, ds, :], hr], axis=0)
        p = jnp.concatenate([PR[q, :, ds, :], hp], axis=0)
        cs = jnp.concatenate([CS[q, :, ds, :], hc], axis=0)
        vel = uc[2] * rinv
        fc = fluxes(uc, vel, p, 2)
        s = jnp.abs(vel) + cs

        def sh(x, k):
            if k == 0:
                return x[:lt]
            y = pltpu.roll(x, (-k) % 128, 2)
            if k > 0:
                return jnp.where(lane >= 128 - k, y[1:], y[:lt])
            prev = jnp.concatenate([y[lt:], y[:lt - 1]], axis=0) if lt > 1 else y[lt:]
            return jnp.where(lane < -k, prev, y[:lt])

        a_cycle = jnp.maximum(s[:lt], sh(s, 1))
        v0 = vel[:lt]
        src = {
            1: k_src * (uc[2][:lt] * v0 + p[:lt]),
            2: -k_src * (uc[1][:lt] * v0),
        }
        ups = []
        for c in range(5):
            up = radial_face(c, r + 3)
            ups.append(up)
            delta = k_low * low_faces[c] - k_up * up
            ff = [sh(fc[c], k) for k in range(-2, 4)]
            uu = [sh(uc[c], k) for k in range(-2, 4)]
            df = [ff[k + 1] - ff[k] for k in range(5)]
            du = [uu[k + 1] - uu[k] for k in range(5)]
            fa = face_flux12(df, du, a_cycle, ff[2] + ff[3])
            fa1 = pltpu.roll(fa, 1, 2)
            ex = pltpu.roll(EX[c], 126 - 8 * lr, 1)[None]
            prev = jnp.concatenate([ex, fa1[:lt - 1]], axis=0) if lt > 1 else ex
            delta = delta - k_cycle * (fa - jnp.where(lane == 0, prev, fa1))
            fx = axial_faces(c, q, base)
            before = jnp.where(sub == 0, pltpu.roll(CX[c, r], 1, 1), pltpu.roll(fx, 1, 1))
            CX[c, r] = fx
            delta = delta - k_line * (fx - before)
            if c in src:
                delta = delta + src[c]
            delta = delta + SECTION_GAIN * uc[c][:lt]
            for l in range(lt):
                ls = slice(128 * l, 128 * l + 128)
                out[c, r, :, ls] = SECTION_KEEP * start[c, r, :, ls] + delta[l]
        return tuple(ups)

    lax.fori_loop(0, nr, one_row, tuple(radial_face(c, 2) for c in range(5)))


def rk_rows(state, lo, hi, left, right, start, r0, r1, share=None, into=None):
    _, rows, stations, cells = state.shape
    lt = cells // 128
    nblk = stations // SB
    q0, q1 = max(r0 - 3, 0), min(r1 + 3, rows)
    nq, nr = q1 - q0, r1 - r0
    whole = into is not None
    cfg = (r0, r1, q0, q1, rows, nblk, lt, whole and into is not False)
    any_spec = pl.BlockSpec(memory_space=pl.ANY)
    halo_spec = pl.BlockSpec((5, stations, 128), lambda i: (0, 0, 0))
    step = r0 // nr
    in_specs = [any_spec, any_spec, any_spec, halo_spec, halo_spec,
                pl.BlockSpec((5, nr, SB, cells), lambda i: (0, step, i, 0))]
    args = [state, lo, hi, left, right, start]
    alias = {}
    if cfg[-1]:
        in_specs.append(any_spec)
        args.append(into)
        alias = {6: 0}
    if whole:
        out_shape = (5, rows, stations, cells)
        out_spec = pl.BlockSpec((5, nr, SB, cells), lambda i: (0, step, i, 0))
    else:
        group = share // SB
        out_shape = (stations // share, 5, nr, share, cells)
        out_spec = pl.BlockSpec(
            (None, 5, nr, SB, cells), lambda i: (i // group, 0, 0, i % group, 0))
    sp = stations + 2 * SB
    f32 = jnp.float32
    field = pltpu.VMEM((nq, lt, sp, 128), f32)
    return pl.pallas_call(
        functools.partial(rk_kernel, cfg),
        out_shape=jax.ShapeDtypeStruct(out_shape, f32),
        grid=(nblk,),
        in_specs=in_specs,
        out_specs=out_spec,
        scratch_shapes=[
            pltpu.VMEM((5, nq, lt, sp, 128), f32),
            pltpu.VMEM((4, nq, lt, sp, 128), f32),
            field, field, field, field,
            pltpu.VMEM((5, 2, nr + 5, lt, SB, 128), f32),
            pltpu.VMEM((nr + 5, lt, SB, 128), f32),
            pltpu.VMEM((5, nr + 5, lt, SB, 128), f32),
            pltpu.VMEM((5, nr, lt, SB, 128), f32),
            pltpu.VMEM((5, SB, 128), f32),
            pltpu.SemaphoreType.DMA((3 * lt,)),
        ],
        input_output_aliases=alias,
        compiler_params=pltpu.CompilerParams(
            dimension_semantics=("arbitrary",), vmem_limit_bytes=56 << 20),
        name="rk_rows_%d_%d" % (r0, r1),
    )(*args)


def merge_kernel(near, smooth, rows_ref, whole, out):
    for j in range(NF):
        keep = j < rows_ref[...]
        for c in range(5):
            out[c, j] = jnp.where(keep, smooth[c, j], near[c, j])


def merge_near(near, smooth, near_rows, whole):
    groups, _, _, share, cells = near.shape
    spec = pl.BlockSpec((None, 5, NF, share, cells), lambda i: (i, 0, 0, 0, 0))
    return pl.pallas_call(
        merge_kernel,
        out_shape=jax.ShapeDtypeStruct(whole.shape, jnp.float32),
        grid=(groups,),
        in_specs=[spec, spec, pl.BlockSpec((share, 1), lambda i: (i, 0)),
                  pl.BlockSpec(memory_space=pl.ANY)],
        out_specs=pl.BlockSpec((5, NF, share, cells), lambda i: (0, 0, i, 0)),
        input_output_aliases={3: 0},
        name="merge_near",
    )(near, smooth, near_rows[:, None], whole)


def edge_kernel(head, tail, out):
    rows = head.shape[1]
    lane = lax.broadcasted_iota(jnp.int32, head.shape[2:], 1)
    for c in range(5):
        acc = jnp.zeros(head.shape[2:], jnp.float32)
        for r in range(rows):
            ends = jnp.where(lane < 64, head[c, r], tail[c, r])
            ends = pltpu.roll(ends, (8 * r + 3) % 128, 1)
            acc = jnp.where((lane >= 8 * r) & (lane < 8 * r + 8), ends, acc)
        out[c] = acc


def azimuthal_edges(state):
    _, rows, stations, cells = state.shape
    sb = 32
    far = cells // 128 - 1
    return pl.pallas_call(
        edge_kernel,
        out_shape=jax.ShapeDtypeStruct((5, stations, rows * 8), jnp.float32),
        grid=(stations // sb,),
        in_specs=[pl.BlockSpec((5, rows, sb, 128), lambda i: (0, 0, i, 0)),
                  pl.BlockSpec((5, rows, sb, 128), lambda i: (0, 0, i, far))],
        out_specs=pl.BlockSpec((5, sb, rows * 8), lambda i: (0, i, 0)),
        name="azimuthal_edges",
    )(state, state)


def mode_tables():
    n = np.arange(NA // 2)[:, None]
    tables = []
    for parity in (0, 1):
        k = np.arange(parity, NA // 4, 2)[None, :]
        angle = 2.0 * math.pi / NA * ((n * k) % NA)
        tables.append(np.concatenate([np.cos(angle), np.sin(angle)], axis=1).astype(np.float32))
    return tables


def low_pass(cycles, cutoffs):
    half = NA // 2
    pieces, shape = cycles.shape[0], cycles.shape[1:]
    x = jnp.transpose(cycles, (1, 2, 3, 0, 4)).reshape(-1, NA)
    parts = (x[:, :half] + x[:, half:], x[:, :half] - x[:, half:])
    back = []
    for parity, table in enumerate(mode_tables()):
        k = np.arange(parity, NA // 4, 2)
        weight = np.where(k == 0, 1.0 / NA, 2.0 / NA).astype(np.float32)
        k2 = jnp.asarray(np.concatenate([k, k]).astype(np.int32))
        w2 = jnp.asarray(np.concatenate([weight, weight]))
        basis = jnp.asarray(table)
        coef = jnp.einsum("rn,nc->rc", parts[parity], basis, precision=lax.Precision.HIGH)
        gains = jnp.where(k2 < cutoffs[..., None], w2, 0.0)
        coef = (coef.reshape(shape[:3] + (-1,)) * gains[None]).reshape(x.shape[0], -1)
        back.append(jnp.einsum("rc,nc->rn", coef, basis, precision=lax.Precision.HIGH))
    y = jnp.concatenate([back[0] + back[1], back[0] - back[1]], axis=1)
    return jnp.transpose(y.reshape(shape[:3] + (pieces, -1)), (3, 0, 1, 2, 4))


def pressure_of(conserved):
    density = conserved[0]
    kinetic = (
        0.5
        * (conserved[1] * conserved[1] + conserved[2] * conserved[2] + conserved[3] * conserved[3])
        / density
    )
    return (HEAT_RATIO - 1.0) * (conserved[4] - kinetic)


def per_device(step_start, section_state, near_rows, cutoff, gore_map):
    _, rows, stations, cells = section_state.shape
    na, nx = lax.axis_size("az"), lax.axis_size("ax")
    cycle_index, line_index = lax.axis_index("az"), lax.axis_index("ax")
    up_a = [(i, (i + 1) % na) for i in range(na)]
    down_a = [((i + 1) % na, i) for i in range(na)]
    up_x = [(i, (i + 1) % nx) for i in range(nx)]
    down_x = [((i + 1) % nx, i) for i in range(nx)]

    edges = azimuthal_edges(section_state)
    from_left = lax.ppermute(edges, "az", up_a)
    right = lax.ppermute(edges, "az", down_a)
    lanes = jnp.arange(rows * 8, dtype=jnp.int32) % 8
    left = jnp.where(lanes < 3, from_left, edges)

    lo = lax.ppermute(section_state[:, :, -3:], "ax", up_x)
    hi = lax.ppermute(section_state[:, :, :3], "ax", down_x)
    lo = jnp.pad(lo, ((0, 0), (0, 0), (SB - 3, 0), (0, 0)), constant_values=1.0)
    hi = jnp.pad(hi, ((0, 0), (0, 0), (0, SB - 3), (0, 0)), constant_values=1.0)

    rest = functools.partial(rk_rows, section_state, lo, hi, left, right, step_start)
    share = stations // na
    near = rest(0, NF, share=share)
    spread = lax.all_to_all(near, "az", 0, 0, tiled=True)
    whole = rest(NF, 2 * NF, into=False)
    spread, whole = lax.optimization_barrier((spread, whole))
    cutoffs = lax.dynamic_slice_in_dim(cutoff, cycle_index * share, share, axis=1)
    kept = low_pass(spread, cutoffs)
    kept, whole = lax.optimization_barrier((kept, whole))
    smooth = lax.all_to_all(kept, "az", 0, 0, tiled=True)
    whole = rest(2 * NF, rows, into=whole)

    canopy = rows // 2
    jump = pressure_of(section_state[:, canopy - 1]) - pressure_of(section_state[:, canopy + 1])
    total = stations * nx
    station = line_index * stations + jnp.arange(stations, dtype=jnp.int32)
    ramp = 1.0 + 2.0 * station.astype(jnp.float32) / total
    weighted = jump * ramp[:, None] * (1.0 / math.sqrt(total * NA / GORES))
    gores = jnp.arange(GORES, dtype=jnp.int32)
    partial = jnp.sum(
        jnp.where(gore_map[None] == gores[:, None, None], weighted[None], 0.0), axis=(1, 2))
    partial, whole = lax.optimization_barrier((partial, whole))
    new_state = merge_near(near, smooth, near_rows, whole)
    gore_loads = lax.psum(partial, ("az", "ax"))
    return (new_state, gore_loads)


def solution(mesh):
    in_specs = (
        P(None, None, "ax", "az"),
        P(None, None, "ax", "az"),
        P("ax"),
        P(None, "ax"),
        P("ax", "az"),
    )
    out_specs = (P(None, None, "ax", "az"), P())
    return jax.shard_map(
        per_device, mesh=mesh, in_specs=in_specs, out_specs=out_specs, check_vma=False
    )
```

time: 604 us -> 314 us (0.52)
  other arithmetic: 366 us -> 3.88 us
  Pallas kernels: 0 us -> 221 us
  waiting for transfers between devices: 106 us -> 12.2 us
  local copies, waits for them, and re-layouts: 42.4 us -> 13.8 us
  matrix products: 24.3 us -> 5.54 us
  between operations: 14.7 us -> 0.85 us
  starting transfers between devices: 7.9 us -> 15.5 us
    pallas_call x0 -> x5, Pallas kernels: none -> 221 us  [the longest x3 209 us: rk_rows(): pl.pallas_call(functools.partial(rk_kernel, cfg), out_shape=jax.ShapeDtyp...]
    add x10 -> x1, other arithmetic: 212 us -> 0.01 us  [per_device(): ramp = 1.0 + 2.0 * station.astype(jnp.float32) / total]
    psum x1 -> x0, waiting for transfers between devices: 106 us -> none  [per_device(): coefficients = lax.psum(partial_modes, 'az')]
    mul x3 -> x1, other arithmetic: 65 us -> 1.47 us  [per_device(): weighted = jump * ramp[:, None] * (1.0 / math.sqrt(total * NA / GORES))]
    unnamed x16 -> x0, other arithmetic: 32.2 us -> none
    concatenate x5 -> x1, other arithmetic: 28.1 us -> 0.29 us  [low_pass(): y = jnp.concatenate([back[0] + back[1], back[0] - back[1]], axis=1)]
    dot_general x2 -> x4, matrix products: 24.3 us -> 5.54 us  [the longest x2 2.85 us: low_pass(): jnp.einsum('rn,nc->rc', parts[parity], basis, precision=lax.Precision.HIGH)]
    slice x11 -> x1, local copies, waits for them, and re-layouts: 16.9 us -> 1.41 us  [per_device(): hi = lax.ppermute(section_state[:, :, :3], 'ax', down_x)]
  transfers between devices with their start and end apart: 5 -> 6, of which waited for: 1 -> 2; matrix products, arithmetic and copies ran while one was open for 35% -> 2% of each run, Pallas kernels for 0% -> 49%
where the time goes in v1:
time: 314 us; the launch traced here: 313 us
  Pallas kernels  221 us (70%)
  blocking collectives  40 us (13%)
  starting transfers between devices  15.5 us (5%)
  local copies, waits for them, and re-layouts  13.8 us (4%)
  waiting for transfers between devices  12.2 us (4%)
  matrix products  5.54 us (2%)
  other arithmetic  3.88 us (1%)
    pallas_call x3, Pallas kernels, rk_rows(): pl.pallas_call(functools.partial(rk_kernel, cfg), out_shape=jax.ShapeDtyp...  209 us
    psum x1, blocking collectives, per_device(): gore_loads = lax.psum(partial, ('az', 'ax'))  40 us
    pallas_call x1, Pallas kernels, merge_near(): pl.pallas_call(merge_kernel, out_shape=jax.ShapeDtypeStruct(whole.shape,...  6.65 us
    ppermute x1, waiting for transfers between devices, per_device(): hi = lax.ppermute(section_state[:, :, :3], 'ax', down_x)  6.62 us
  transfers between devices with their start and end apart: 6, of which 2 were waited for; matrix products, arithmetic and copies ran while one was open for 2% of the time, Pallas kernels for 49%

profile of v1, /device:TPU:0, one launch (start us, length us, event | category | flops | bytes accessed | tf_op | source)
XLA Modules:
  0.0 313.2 jit_solution(3641532442890746717)
XLA Ops:
  0.6 0.0 copy-start
  0.6 6.1 %azimuthal_edges.1 = f32[5,128,128]{2,1,0:T(8,128)} custom-call(f32[5,16,128,256]{3,2,1,0:T(8,128)} %refs_0_.5, f32[5,16,128,256]{3,2,1,0:T(8,128)} %refs_0_.5), custom_call_target="tpu_custom_call" | custom-call | tf_op jit(solution)/shard_map/azimuthal_edges/pallas_call | solution.py:363
  6.7 0.5 collective-permute-start.2
  7.2 1.4 fusion.16
  8.6 2.7 collective-permute-start
  11.3 2.1 collective-permute-start.1
  13.3 2.3 collective-permute-start.3
  15.7 5.5 %collective-permute-done = f32[5,16,3,256]{3,2,1,0:T(4,128)S(1)} collective-permute-done((f32[5,16,3,256]{3,2,1,0:T(4,128)S(1)}, f32[5,16,3,256]{3,2,1,0:T(4,128)S(1)}, u32[]{:S(2)}, u32[]{:S(2)}) %collective-permute-start) | collective-permute-done | bytes 245792 | tf_op jit(solution)/shard_map/ppermute | solution.py:429
  21.2 0.9 pad.8.refs_1_
  22.1 6.6 %collective-permute-done.1 = f32[5,16,3,256]{3,2,1,0:T(4,128)S(1)} collective-permute-done((f32[5,16,3,256]{3,2,1,0:T(4,128)S(1)}, f32[5,16,3,256]{3,2,1,0:T(4,128)S(1)}, u32[]{:S(2)}, u32[]{:S(2)}) %collective-permute-start.1) | collective-permute-done | bytes 245792 | tf_op jit(solution)/shard_map/ppermute | solution.py:430
  28.8 0.9 pad.9.refs_2_
  29.7 0.0 collective-permute-done.2
  29.7 0.8 broadcast_select_fusion.refs_3_
  30.4 0.0 collective-permute-done.3.refs_4_
  30.4 0.7 copy-done.5
  31.2 54.9 %rk_rows_0_4.1.near = f32[8,5,4,16,256]{4,3,2,1,0:T(8,128)} custom-call(f32[5,16,128,256]{3,2,1,0:T(8,128)} %refs_0_.5, f32[5,16,8,256]{3,2,1,0:T(8,128)} %pad.8.refs_1_, f32[5,16,8,256]{3,2,1,0:T(8,128)} %pad.9.refs_2_, f32[5,128,128]{2,1,0:T(8,128)} %broadcast_select_fusion.refs_3_, f32[5,128,128]{2,1,0:T(8,128)} %copy-done.5, f32[5,16,128,256]{3,2,1,0:T(8,128)} %refs_5_.5), custom_call_target="tpu_custom_call" | custom-call | tf_op jit(solution)/shard_map/rk_rows_0_4/pallas_call | solution.py:301
  86.1 0.0 copy-start.8
  86.1 0.0 copy-start.9
  86.1 0.0 copy-start.10
  86.1 4.0 %all-to-all-start = ((f32[8,5,4,16,256]{4,3,2,1,0:T(8,128)}), f32[8,5,4,16,256]{4,3,2,1,0:T(8,128)S(1)}, u32[]{:S(2)}, u32[]{:S(2)}) async-start(f32[8,5,4,16,256]{4,3,2,1,0:T(8,128)} %rk_rows_0_4.1.near), calls=%async_computation | async-start | bytes 5242880 | tf_op jit(solution)/shard_map/all_to_all | solution.py:437
  90.1 0.1 constant_dynamic-slice_fusion
  90.2 0.1 compare_select_fusion
  90.3 56.5 %rk_rows_4_8.1.refs_6_ = f32[5,16,128,256]{3,2,1,0:T(8,128)} custom-call(f32[5,16,128,256]{3,2,1,0:T(8,128)} %refs_0_.5, f32[5,16,8,256]{3,2,1,0:T(8,128)} %pad.8.refs_1_, f32[5,16,8,256]{3,2,1,0:T(8,128)} %pad.9.refs_2_, f32[5,128,128]{2,1,0:T(8,128)} %broadcast_select_fusion.refs_3_, f32[5,128,128]{2,1,0:T(8,128)} %copy-done.5, f32[5,16,128,256]{3,2,1,0:T(8,128)} %refs_5_.5), custom_call_target="tpu_custom_call" | custom-call | tf_op jit(solution)/shard_map/rk_rows_4_8/pallas_call | solution.py:301
  146.8 0.0 all-to-all-done
  146.8 2.2 copy.19
  149.0 0.0 copy-start.4
  149.0 1.2 copy.22
  150.1 0.1 mul.139
  150.2 0.3 copy-done.4
  150.6 1.4 fusion.7
  152.0 0.0 copy-start.3
  152.0 1.3 fusion.18
  153.4 0.1 mul.136
  153.4 0.2 copy-done.3
  153.6 1.4 fusion.4
  155.0 1.4 fusion.17
  156.4 0.3 pad_maximum_fusion
  156.7 1.1 copy.23
  157.8 2.3 copy.25
  160.2 4.1 %all-to-all-start.1 = ((f32[8,5,4,16,256]{4,3,2,1,0:T(8,128)}), f32[8,5,4,16,256]{4,3,2,1,0:T(8,128)S(1)}, u32[]{:S(2)}, u32[]{:S(2)}) async-start(f32[8,5,4,16,256]{4,3,2,1,0:T(8,128)} %bitcast.26), calls=%async_computation.1 | async-start | bytes 5242880 | tf_op jit(solution)/shard_map/all_to_all | solution.py:443
  164.2 0.7 copy.21.rows_ref
  165.0 1.5 fusion.14
  166.5 1.3 select_reduce_fusion
  167.7 97.3 %rk_rows_8_16.1.whole = f32[5,16,128,256]{3,2,1,0:T(8,128)} custom-call(f32[5,16,128,256]{3,2,1,0:T(8,128)} %refs_0_.5, f32[5,16,8,256]{3,2,1,0:T(8,128)} %pad.8.refs_1_, f32[5,16,8,256]{3,2,1,0:T(8,128)} %pad.9.refs_2_, f32[5,128,128]{2,1,0:T(8,128)} %broadcast_select_fusion.refs_3_, f32[5,128,128]{2,1,0:T(8,128)} %copy-done.5, ...), custom_call_target="tpu_custom_call", output_to_operand_aliasing={{}: (6, {})} | custom-call | tf_op jit(solution)/shard_map/rk_rows_8_16/pallas_call | solution.py:301
  265.0 40.0 %psum.7 = f32[80]{0:T(128)} all-reduce(f32[80]{0:T(128)S(1)} %select_reduce_fusion), channel_id=1, replica_groups=mesh['az'=8,'ax'=4] {'az','ax'}, use_global_device_ids=true, to_apply=%region_1.2 | all-reduce | flops 80 | bytes 640 | tf_op jit(solution)/shard_map/psum | solution.py:457
  305.0 0.0 all-to-all-done.1.smooth
  305.0 1.5 copy-done.2
  306.6 6.7 %merge_near.1 = f32[5,16,128,256]{3,2,1,0:T(8,128)} custom-call(f32[8,5,4,16,256]{4,3,2,1,0:T(8,128)} %rk_rows_0_4.1.near, f32[8,5,4,16,256]{4,3,2,1,0:T(8,128)} %copy-done.2, s32[128,1]{1,0:T(8,128)} %copy.21.rows_ref, f32[5,16,128,256]{3,2,1,0:T(8,128)} %rk_rows_8_16.1.whole), custom_call_target="tpu_custom_call", output_to_operand_aliasing={{}: (3, {})} | custom-call | tf_op jit(solution)/shard_map/merge_near/pallas_call | solution.py:335
  (16 shorter events, 0.0 us)
Async XLA Ops:
  0.6 89.5 %copy-start = (s32[4,128]{1,0:T(4,128)S(1)}, s32[4,128]{1,0:T(4,128)}, u32[]{:S(2)}) copy-start(s32[4,128]{1,0:T(4,128)} %param.14) | copy-start | bytes 6148
  6.7 23.0 %copy-start.6 = (f32[5,128,128]{2,1,0:T(8,128)S(1)}, f32[5,128,128]{2,1,0:T(8,128)}, u32[]{:S(2)}) copy-start(f32[5,128,128]{2,1,0:T(8,128)} %azimuthal_edges.1) | copy-start | bytes 983044
  6.7 23.0 %collective-permute-start.2 = (f32[5,128,128]{2,1,0:T(8,128)}, f32[5,128,128]{2,1,0:T(8,128)S(1)}, u32[]{:S(2)}, u32[]{:S(2)}) collective-permute-start(f32[5,128,128]{2,1,0:T(8,128)} %azimuthal_edges.1), channel_id=1, source_target_pairs={{0,4},{4,8},{8,12},{12,16},{16,20},{20,24},{24,28},{28,0},{1,5},{5... | collective-permute-start | bytes 983048 | tf_op jit(solution)/shard_map/ppermute | solution.py:424
  8.6 12.6 %collective-permute-start = (f32[5,16,3,256]{3,2,1,0:T(4,128)S(1)}, f32[5,16,3,256]{3,2,1,0:T(4,128)S(1)}, u32[]{:S(2)}, u32[]{:S(2)}) collective-permute-start(f32[5,16,3,256]{3,2,1,0:T(4,128)S(1)} %get-tuple-element.15), channel_id=1, source_target_pairs={{0,1},{1,2},{2,3},{3,0},{4,5},{5,6},{6,7},{7,4},{8,9},{9,10},{10,1... | collective-permute-start | bytes 737288 | tf_op jit(solution)/shard_map/ppermute | solution.py:429
  11.3 17.5 %collective-permute-start.1 = (f32[5,16,3,256]{3,2,1,0:T(4,128)S(1)}, f32[5,16,3,256]{3,2,1,0:T(4,128)S(1)}, u32[]{:S(2)}, u32[]{:S(2)}) collective-permute-start(f32[5,16,3,256]{3,2,1,0:T(4,128)S(1)} %get-tuple-element.14), channel_id=1, source_target_pairs={{1,0},{2,1},{3,2},{0,3},{5,4},{6,5},{7,6},{4,7},{9,8},{10,9},{11,1... | collective-permute-start | bytes 737288 | tf_op jit(solution)/shard_map/ppermute | solution.py:430
  13.3 17.1 %collective-permute-start.3 = (f32[5,128,128]{2,1,0:T(8,128)}, f32[5,128,128]{2,1,0:T(8,128)S(1)}, u32[]{:S(2)}, u32[]{:S(2)}) collective-permute-start(f32[5,128,128]{2,1,0:T(8,128)} %azimuthal_edges.1), channel_id=1, source_target_pairs={{4,0},{8,4},{12,8},{16,12},{20,16},{24,20},{28,24},{0,28},{5,1},{9... | collective-permute-start | bytes 983048 | tf_op jit(solution)/shard_map/ppermute | solution.py:425
  30.4 0.7 copy-start.5
  86.1 4.1 %copy-start.8 = (s32[512]{0:T(512)S(1)}, s32[512]{0:T(512)}, u32[]{:S(2)}) copy-start(s32[512]{0:T(512)} %constant.60.clone) | copy-start | bytes 6148
  86.1 4.1 %copy-start.9 = (f32[512]{0:T(512)S(1)}, f32[512]{0:T(512)}, u32[]{:S(2)}) copy-start(f32[512]{0:T(512)} %constant.61.clone) | copy-start | bytes 6148
  86.1 4.1 %copy-start.10 = (s32[512]{0:T(512)S(1)}, s32[512]{0:T(512)}, u32[]{:S(2)}) copy-start(s32[512]{0:T(512)} %constant.63.clone) | copy-start | bytes 6148
  86.1 60.6 %all-to-all-start = ((f32[8,5,4,16,256]{4,3,2,1,0:T(8,128)}), f32[8,5,4,16,256]{4,3,2,1,0:T(8,128)S(1)}, u32[]{:S(2)}, u32[]{:S(2)}) async-start(f32[8,5,4,16,256]{4,3,2,1,0:T(8,128)} %rk_rows_0_4.1.near), calls=%async_computation | async-start | bytes 5242880 | tf_op jit(solution)/shard_map/all_to_all | solution.py:437
  149.0 1.6 copy-start.4
  152.0 1.6 copy-start.3
  160.2 4.1 %copy-start.11 = (s32[128]{0:T(128)S(1)}, s32[128]{0:T(128)}, u32[]{:S(2)}) copy-start(s32[128]{0:T(128)} %param.13) | copy-start | bytes 1540
  160.2 6.3 %copy-start.7 = (s32[128,256]{1,0:T(8,128)S(1)}, s32[128,256]{1,0:T(8,128)}, u32[]{:S(2)}) copy-start(s32[128,256]{1,0:T(8,128)} %param.15) | copy-start | bytes 393220
  160.2 144.9 %all-to-all-start.1 = ((f32[8,5,4,16,256]{4,3,2,1,0:T(8,128)}), f32[8,5,4,16,256]{4,3,2,1,0:T(8,128)S(1)}, u32[]{:S(2)}, u32[]{:S(2)}) async-start(f32[8,5,4,16,256]{4,3,2,1,0:T(8,128)} %bitcast.26), calls=%async_computation.1 | async-start | bytes 5242880 | tf_op jit(solution)/shard_map/all_to_all | solution.py:443
  305.0 1.5 copy-start.2
  306.5 6.7 %copy-start.1 = (s32[4,128]{1,0:T(4,128)S(1)}, s32[4,128]{1,0:T(4,128)}, u32[]{:S(2)}) copy-start(s32[4,128]{1,0:T(4,128)} %param.14) | copy-start | bytes 6148

commit v2 on v1

--- a/solution.py
+++ b/solution.py
@@ -433,16 +433,6 @@
 
     rest = functools.partial(rk_rows, section_state, lo, hi, left, right, step_start)
     share = stations // na
-    near = rest(0, NF, share=share)
-    spread = lax.all_to_all(near, "az", 0, 0, tiled=True)
-    whole = rest(NF, 2 * NF, into=False)
-    spread, whole = lax.optimization_barrier((spread, whole))
-    cutoffs = lax.dynamic_slice_in_dim(cutoff, cycle_index * share, share, axis=1)
-    kept = low_pass(spread, cutoffs)
-    kept, whole = lax.optimization_barrier((kept, whole))
-    smooth = lax.all_to_all(kept, "az", 0, 0, tiled=True)
-    whole = rest(2 * NF, rows, into=whole)
-
     canopy = rows // 2
     jump = pressure_of(section_state[:, canopy - 1]) - pressure_of(section_state[:, canopy + 1])
     total = stations * nx
@@ -452,9 +442,21 @@
     gores = jnp.arange(GORES, dtype=jnp.int32)
     partial = jnp.sum(
         jnp.where(gore_map[None] == gores[:, None, None], weighted[None], 0.0), axis=(1, 2))
-    partial, whole = lax.optimization_barrier((partial, whole))
+    parts = jnp.broadcast_to(jnp.pad(partial, (0, 128 - GORES)), (na * nx, 128))
+    parts = lax.all_to_all(parts, ("az", "ax"), 0, 0, tiled=True)
+    near = rest(0, NF, share=share)
+    parts, near = lax.optimization_barrier((parts, near))
+    spread = lax.all_to_all(near, "az", 0, 0, tiled=True)
+    whole = rest(NF, 2 * NF, into=False)
+    spread, whole = lax.optimization_barrier((spread, whole))
+    cutoffs = lax.dynamic_slice_in_dim(cutoff, cycle_index * share, share, axis=1)
+    kept = low_pass(spread, cutoffs)
+    kept, whole = lax.optimization_barrier((kept, whole))
+    smooth = lax.all_to_all(kept, "az", 0, 0, tiled=True)
+    whole = rest(2 * NF, rows, into=whole)
+
+    gore_loads = jnp.sum(parts, axis=0)[:GORES]
     new_state = merge_near(near, smooth, near_rows, whole)
-    gore_loads = lax.psum(partial, ("az", "ax"))
     return (new_state, gore_loads)
 
 

time: 314 us -> 272 us (0.87)
  blocking collectives: 40 us -> 0 us
  waiting for transfers between devices: 12.2 us -> 5.7 us
  starting transfers between devices: 15.5 us -> 19.1 us
    psum x1 -> x0, blocking collectives: 40 us -> none  [per_device(): gore_loads = lax.psum(partial, ('az', 'ax'))]
    ppermute x1, waiting for transfers between devices: 5.52 us -> 1.91 us  [per_device(): lo = lax.ppermute(section_state[:, :, -3:], 'ax', up_x)]
    all_to_all x0 -> x1, starting transfers between devices: none -> 3.31 us  [per_device(): parts = lax.all_to_all(parts, ('az', 'ax'), 0, 0, tiled=True)]
  transfers between devices with their start and end apart: 6 -> 7, of which waited for: 2 -> 2; matrix products, arithmetic and copies ran while one was open for 2% -> 3% of each run, Pallas kernels for 49% -> 77%
where the time goes in v2:
time: 272 us; the launch traced here: 271 us
  Pallas kernels  221 us (81%)
  starting transfers between devices  19.1 us (7%)
  local copies, waits for them, and re-layouts  14.4 us (5%)
  waiting for transfers between devices  5.7 us (2%)
  matrix products  5.54 us (2%)
  other arithmetic  4.41 us (2%)
    pallas_call x3, Pallas kernels, rk_rows(): pl.pallas_call(functools.partial(rk_kernel, cfg), out_shape=jax.ShapeDtyp...  209 us
    pallas_call x1, Pallas kernels, merge_near(): pl.pallas_call(merge_kernel, out_shape=jax.ShapeDtypeStruct(whole.shape,...  6.65 us
    pallas_call x1, Pallas kernels, azimuthal_edges(): pl.pallas_call(edge_kernel, out_shape=jax.ShapeDtypeStruct((5, stations,...  6.07 us
  transfers between devices with their start and end apart: 7, of which 2 were waited for; matrix products, arithmetic and copies ran while one was open for 3% of the time, Pallas kernels for 77%

profile of v2, /device:TPU:0, one launch (start us, length us, event | category | flops | bytes accessed | tf_op | source)
XLA Modules:
  0.0 271.5 jit_solution(3351658720490338779)
XLA Ops:
  0.6 0.0 copy-start
  0.6 6.1 %azimuthal_edges.1 = f32[5,128,128]{2,1,0:T(8,128)} custom-call(f32[5,16,128,256]{3,2,1,0:T(8,128)} %refs_0_.5, f32[5,16,128,256]{3,2,1,0:T(8,128)} %refs_0_.5), custom_call_target="tpu_custom_call" | custom-call | tf_op jit(solution)/shard_map/azimuthal_edges/pallas_call | solution.py:363
  6.7 0.5 collective-permute-start.2
  7.2 2.9 %collective-permute-start.3 = (f32[5,128,128]{2,1,0:T(8,128)}, f32[5,128,128]{2,1,0:T(8,128)S(1)}, u32[]{:S(2)}, u32[]{:S(2)}) collective-permute-start(f32[5,128,128]{2,1,0:T(8,128)} %azimuthal_edges.1), channel_id=1, source_target_pairs={{4,0},{8,4},{12,8},{16,12},{20,16},{24,20},{28,24},{0,28},{5,1},{9... | collective-permute-start | bytes 983048 | tf_op jit(solution)/shard_map/ppermute | solution.py:425
  10.1 1.4 fusion.16
  11.5 0.0 copy-start.6
  11.5 2.3 collective-permute-start
  13.9 2.1 collective-permute-start.1
  16.0 1.5 fusion.14
  17.4 1.3 select_reduce_fusion
  18.7 0.6 broadcast_in_dim.46
  19.3 3.3 %all-to-all-start = ((f32[32,1,128]{2,1,0:T(1,128)}), f32[32,1,128]{2,1,0:T(1,128)S(1)}, u32[]{:S(2)}, u32[]{:S(2)}) async-start(f32[32,1,128]{2,1,0:T(1,128)} %broadcast_in_dim.46), calls=%async_computation | async-start | bytes 32768 | tf_op jit(solution)/shard_map/all_to_all | solution.py:446
  22.7 1.9 collective-permute-done
  24.6 0.9 pad.13.refs_1_
  25.5 3.8 %collective-permute-done.1 = f32[5,16,3,256]{3,2,1,0:T(4,128)S(1)} collective-permute-done((f32[5,16,3,256]{3,2,1,0:T(4,128)S(1)}, f32[5,16,3,256]{3,2,1,0:T(4,128)S(1)}, u32[]{:S(2)}, u32[]{:S(2)}) %collective-permute-start.1) | collective-permute-done | bytes 245792 | tf_op jit(solution)/shard_map/ppermute | solution.py:430
  29.3 0.9 pad.14.refs_2_
  30.2 0.0 collective-permute-done.2
  30.2 0.8 broadcast_select_fusion.refs_3_
  30.9 0.7 copy-done.5
  31.7 54.9 %rk_rows_0_4.1.near = f32[8,5,4,16,256]{4,3,2,1,0:T(8,128)} custom-call(f32[5,16,128,256]{3,2,1,0:T(8,128)} %refs_0_.5, f32[5,16,8,256]{3,2,1,0:T(8,128)} %pad.13.refs_1_, f32[5,16,8,256]{3,2,1,0:T(8,128)} %pad.14.refs_2_, f32[5,128,128]{2,1,0:T(8,128)} %broadcast_select_fusion.refs_3_, f32[5,128,128]{2,1,0:T(8,128)} %copy-done.5, f32[5,16,128,256]{3,2,1,0:T(8,128)} %refs_5_.5), custom_call_target="tpu_custom_call" | custom-call | tf_op jit(solution)/shard_map/rk_rows_0_4/pallas_call | solution.py:301
  86.6 0.0 copy-start.8
  86.6 0.0 copy-start.9
  86.6 0.0 copy-start.10
  86.6 4.0 %all-to-all-start.1 = ((f32[8,5,4,16,256]{4,3,2,1,0:T(8,128)}), f32[8,5,4,16,256]{4,3,2,1,0:T(8,128)S(1)}, u32[]{:S(2)}, u32[]{:S(2)}) async-start(f32[8,5,4,16,256]{4,3,2,1,0:T(8,128)} %rk_rows_0_4.1.near), calls=%async_computation.1 | async-start | bytes 5242880 | tf_op jit(solution)/shard_map/all_to_all | solution.py:449
  90.6 0.1 constant_dynamic-slice_fusion
  90.7 0.1 compare_select_fusion
  90.8 56.5 %rk_rows_4_8.1.refs_6_ = f32[5,16,128,256]{3,2,1,0:T(8,128)} custom-call(f32[5,16,128,256]{3,2,1,0:T(8,128)} %refs_0_.5, f32[5,16,8,256]{3,2,1,0:T(8,128)} %pad.13.refs_1_, f32[5,16,8,256]{3,2,1,0:T(8,128)} %pad.14.refs_2_, f32[5,128,128]{2,1,0:T(8,128)} %broadcast_select_fusion.refs_3_, f32[5,128,128]{2,1,0:T(8,128)} %copy-done.5, f32[5,16,128,256]{3,2,1,0:T(8,128)} %refs_5_.5), custom_call_target="tpu_custom_call" | custom-call | tf_op jit(solution)/shard_map/rk_rows_4_8/pallas_call | solution.py:301
  147.3 2.2 copy.19
  149.5 0.0 copy-start.4
  149.5 1.2 copy.22
  150.6 0.1 mul.156
  150.7 0.3 copy-done.4
  151.1 1.4 fusion.7
  152.5 0.0 copy-start.3
  152.5 1.3 fusion.18
  153.9 0.1 mul.153
  153.9 0.2 copy-done.3
  154.1 1.4 fusion.4
  155.5 1.4 fusion.17
  156.9 0.3 pad_maximum_fusion
  157.2 1.1 copy.23
  158.3 2.3 copy.25
  160.7 4.1 %all-to-all-start.2 = ((f32[8,5,4,16,256]{4,3,2,1,0:T(8,128)}), f32[8,5,4,16,256]{4,3,2,1,0:T(8,128)S(1)}, u32[]{:S(2)}, u32[]{:S(2)}) async-start(f32[8,5,4,16,256]{4,3,2,1,0:T(8,128)} %bitcast.28), calls=%async_computation.2 | async-start | bytes 5242880 | tf_op jit(solution)/shard_map/all_to_all | solution.py:455
  164.7 0.7 copy.21.rows_ref
  165.5 0.5 reduce_sum.19
  166.0 97.3 %rk_rows_8_16.1.whole = f32[5,16,128,256]{3,2,1,0:T(8,128)} custom-call(f32[5,16,128,256]{3,2,1,0:T(8,128)} %refs_0_.5, f32[5,16,8,256]{3,2,1,0:T(8,128)} %pad.13.refs_1_, f32[5,16,8,256]{3,2,1,0:T(8,128)} %pad.14.refs_2_, f32[5,128,128]{2,1,0:T(8,128)} %broadcast_select_fusion.refs_3_, f32[5,128,128]{2,1,0:T(8,128)} %copy-done.5, ...), custom_call_target="tpu_custom_call", output_to_operand_aliasing={{}: (6, {})} | custom-call | tf_op jit(solution)/shard_map/rk_rows_8_16/pallas_call | solution.py:301
  263.3 1.5 copy-done.2
  264.8 6.7 %merge_near.1 = f32[5,16,128,256]{3,2,1,0:T(8,128)} custom-call(f32[8,5,4,16,256]{4,3,2,1,0:T(8,128)} %rk_rows_0_4.1.near, f32[8,5,4,16,256]{4,3,2,1,0:T(8,128)} %copy-done.2, s32[128,1]{1,0:T(8,128)} %copy.21.rows_ref, f32[5,16,128,256]{3,2,1,0:T(8,128)} %rk_rows_8_16.1.whole), custom_call_target="tpu_custom_call", output_to_operand_aliasing={{}: (3, {})} | custom-call | tf_op jit(solution)/shard_map/merge_near/pallas_call | solution.py:335
  (20 shorter events, 0.1 us)
Async XLA Ops:
  0.6 90.0 %copy-start = (s32[4,128]{1,0:T(4,128)S(1)}, s32[4,128]{1,0:T(4,128)}, u32[]{:S(2)}) copy-start(s32[4,128]{1,0:T(4,128)} %param.14) | copy-start | bytes 6148
  6.7 10.7 %copy-start.7 = (s32[128,256]{1,0:T(8,128)S(1)}, s32[128,256]{1,0:T(8,128)}, u32[]{:S(2)}) copy-start(s32[128,256]{1,0:T(8,128)} %param.15) | copy-start | bytes 393220
  6.7 23.5 %collective-permute-start.2 = (f32[5,128,128]{2,1,0:T(8,128)}, f32[5,128,128]{2,1,0:T(8,128)S(1)}, u32[]{:S(2)}, u32[]{:S(2)}) collective-permute-start(f32[5,128,128]{2,1,0:T(8,128)} %azimuthal_edges.1), channel_id=1, source_target_pairs={{0,4},{4,8},{8,12},{12,16},{16,20},{20,24},{24,28},{28,0},{1,5},{5... | collective-permute-start | bytes 983048 | tf_op jit(solution)/shard_map/ppermute | solution.py:424
  7.2 23.8 %collective-permute-start.3 = (f32[5,128,128]{2,1,0:T(8,128)}, f32[5,128,128]{2,1,0:T(8,128)S(1)}, u32[]{:S(2)}, u32[]{:S(2)}) collective-permute-start(f32[5,128,128]{2,1,0:T(8,128)} %azimuthal_edges.1), channel_id=1, source_target_pairs={{4,0},{8,4},{12,8},{16,12},{20,16},{24,20},{28,24},{0,28},{5,1},{9... | collective-permute-start | bytes 983048 | tf_op jit(solution)/shard_map/ppermute | solution.py:425
  11.5 18.7 %copy-start.6 = (f32[5,128,128]{2,1,0:T(8,128)S(1)}, f32[5,128,128]{2,1,0:T(8,128)}, u32[]{:S(2)}) copy-start(f32[5,128,128]{2,1,0:T(8,128)} %azimuthal_edges.1) | copy-start | bytes 983044
  11.5 13.0 %collective-permute-start = (f32[5,16,3,256]{3,2,1,0:T(4,128)S(1)}, f32[5,16,3,256]{3,2,1,0:T(4,128)S(1)}, u32[]{:S(2)}, u32[]{:S(2)}) collective-permute-start(f32[5,16,3,256]{3,2,1,0:T(4,128)S(1)} %get-tuple-element.15), channel_id=1, source_target_pairs={{0,1},{1,2},{2,3},{3,0},{4,5},{5,6},{6,7},{7,4},{8,9},{9,10},{10,1... | collective-permute-start | bytes 737288 | tf_op jit(solution)/shard_map/ppermute | solution.py:429
  13.9 15.4 %collective-permute-start.1 = (f32[5,16,3,256]{3,2,1,0:T(4,128)S(1)}, f32[5,16,3,256]{3,2,1,0:T(4,128)S(1)}, u32[]{:S(2)}, u32[]{:S(2)}) collective-permute-start(f32[5,16,3,256]{3,2,1,0:T(4,128)S(1)} %get-tuple-element.14), channel_id=1, source_target_pairs={{1,0},{2,1},{3,2},{0,3},{5,4},{6,5},{7,6},{4,7},{9,8},{10,9},{11,1... | collective-permute-start | bytes 737288 | tf_op jit(solution)/shard_map/ppermute | solution.py:430
  19.3 67.3 %all-to-all-start = ((f32[32,1,128]{2,1,0:T(1,128)}), f32[32,1,128]{2,1,0:T(1,128)S(1)}, u32[]{:S(2)}, u32[]{:S(2)}) async-start(f32[32,1,128]{2,1,0:T(1,128)} %broadcast_in_dim.46), calls=%async_computation | async-start | bytes 32768 | tf_op jit(solution)/shard_map/all_to_all | solution.py:446
  30.9 0.7 copy-start.5
  86.6 4.1 %copy-start.8 = (s32[512]{0:T(512)S(1)}, s32[512]{0:T(512)}, u32[]{:S(2)}) copy-start(s32[512]{0:T(512)} %constant.61.clone) | copy-start | bytes 6148
  86.6 4.1 %copy-start.9 = (f32[512]{0:T(512)S(1)}, f32[512]{0:T(512)}, u32[]{:S(2)}) copy-start(f32[512]{0:T(512)} %constant.62.clone) | copy-start | bytes 6148
  86.6 4.1 %copy-start.10 = (s32[512]{0:T(512)S(1)}, s32[512]{0:T(512)}, u32[]{:S(2)}) copy-start(s32[512]{0:T(512)} %constant.64.clone) | copy-start | bytes 6148
  86.6 60.6 %all-to-all-start.1 = ((f32[8,5,4,16,256]{4,3,2,1,0:T(8,128)}), f32[8,5,4,16,256]{4,3,2,1,0:T(8,128)S(1)}, u32[]{:S(2)}, u32[]{:S(2)}) async-start(f32[8,5,4,16,256]{4,3,2,1,0:T(8,128)} %rk_rows_0_4.1.near), calls=%async_computation.1 | async-start | bytes 5242880 | tf_op jit(solution)/shard_map/all_to_all | solution.py:449
  149.5 1.6 copy-start.4
  152.5 1.6 copy-start.3
  160.7 4.1 %copy-start.11 = (s32[128]{0:T(128)S(1)}, s32[128]{0:T(128)}, u32[]{:S(2)}) copy-start(s32[128]{0:T(128)} %param.13) | copy-start | bytes 1540
  160.7 102.6 %all-to-all-start.2 = ((f32[8,5,4,16,256]{4,3,2,1,0:T(8,128)}), f32[8,5,4,16,256]{4,3,2,1,0:T(8,128)S(1)}, u32[]{:S(2)}, u32[]{:S(2)}) async-start(f32[8,5,4,16,256]{4,3,2,1,0:T(8,128)} %bitcast.28), calls=%async_computation.2 | async-start | bytes 5242880 | tf_op jit(solution)/shard_map/all_to_all | solution.py:455
  263.3 1.5 copy-start.2
  264.8 6.7 %copy-start.1 = (s32[4,128]{1,0:T(4,128)S(1)}, s32[4,128]{1,0:T(4,128)}, u32[]{:S(2)}) copy-start(s32[4,128]{1,0:T(4,128)} %param.14) | copy-start | bytes 6148
